TPU v7x, 32 devices: a whole 2x2x4 slice. The times are simulated.
32 devices in a mesh: expert: 4 (over y, core), dp: 8 (over z, x).
Axes of the slice: x: 2, y: 2, z: 4, core: 2. Of those that a mesh axis runs over, the one named last changes fastest.
Arguments:
- tokens: bfloat16 [4096, 1024], P(('expert', 'dp')), may hold values from -6 to 6
- d_output: bfloat16 [4096, 1024], P(('expert', 'dp')), may hold values from -6 to 6
- expert_ids: int32 [4096, 8], P(('expert', 'dp')), may hold values from 0 to 127, as said below
- gate_scores: bfloat16 [4096, 8], P(('expert', 'dp')), may hold values from 0.099609375 to 1
- gate_up_w: bfloat16 [4, 1024, 768], P('expert', 'dp'), may hold values from -0.1875 to 0.1875
- down_w: bfloat16 [4, 1024, 384], P('expert', 'dp'), may hold values from -0.3125 to 0.3125
Outputs:
- d_tokens: bfloat16 [4096, 1024], P(('expert', 'dp'))
- d_gates: bfloat16 [4096, 8], P(('expert', 'dp'))
- d_down: float32 [4, 1024, 384], P('expert', 'dp')
Inputs may be any that keep to these rules, and one draw needn't show every extreme that they name: `expert_ids`: each token names 8 different experts. The tokens of one device name no expert more than 12 times, and in every draw one expert below 4 is named exactly 12 times by the tokens of every device.
All inputs are finite; a program needn't handle non-finite values.
Results may differ from a plain program's by a relative error of at most 0.0062.
Values may be sent and summed in bfloat16 or wider, within the bound.
A program may use at most 64 MiB of HBM per device.

v0:
```python
import jax
import jax.numpy as jnp
from jax import lax
from jax.sharding import PartitionSpec as P

TOPK = 8
CAP = 12


def transpose_product(left, right):
    return lax.dot_general(
        left, right, (((0,), (0,)), ((), ())), preferred_element_type=jnp.float32
    )


def product_transposed(left, right):
    return lax.dot_general(
        left, right, (((1,), (1,)), ((), ())), preferred_element_type=jnp.float32
    )


def on_device(tokens, d_output, expert_ids, gate_scores, gate_up_w, down_w):
    gate_full, down_full = (
        lax.all_gather(gate_up_w, "dp", axis=1, tiled=True),
        lax.all_gather(down_w, "dp", axis=1, tiled=True),
    )
    gate_full = gate_full[0]
    down_full = down_full[0]
    groups = lax.axis_size("expert")
    slot_count = groups * CAP
    tok_rows = tokens.shape[0]
    features = tokens.shape[1]
    width = down_w.shape[2]
    flat_ids = expert_ids.reshape(-1)
    entries = flat_ids.shape[0]
    one_hot = (flat_ids[:, None] == jnp.arange(groups, dtype=jnp.int32)[None, :]).astype(jnp.int32)
    earlier = jnp.cumsum(one_hot, axis=0) - one_hot
    within = jnp.sum(earlier * one_hot, axis=1)
    inside = flat_ids < groups
    slot_of = jnp.where(inside, flat_ids * CAP + within, slot_count)
    owner = (
        jnp.full((slot_count,), -1, jnp.int32)
        .at[slot_of]
        .set(jnp.arange(entries, dtype=jnp.int32), mode="drop")
    )
    filled = owner >= 0
    source = jnp.maximum(owner, 0)
    token_of = jnp.where(filled, source // TOPK, -1)
    picker = (token_of[:, None] == jnp.arange(tok_rows, dtype=jnp.int32)[None, :]).astype(
        jnp.bfloat16
    )
    send_inputs = jnp.dot(picker, tokens, preferred_element_type=jnp.float32).astype(jnp.bfloat16)
    send_upstream = jnp.dot(picker, d_output, preferred_element_type=jnp.float32).astype(
        jnp.bfloat16
    )
    send_gates = jnp.where(filled, gate_scores.reshape(-1)[source], jnp.zeros((), jnp.bfloat16))
    recv_inputs, recv_upstream, recv_gates = (
        lax.all_to_all(
            send_inputs.reshape(groups, CAP, features),
            "expert",
            split_axis=0,
            concat_axis=0,
            tiled=True,
        ),
        lax.all_to_all(
            send_upstream.reshape(groups, CAP, features),
            "expert",
            split_axis=0,
            concat_axis=0,
            tiled=True,
        ),
        lax.all_to_all(
            send_gates.reshape(groups, CAP), "expert", split_axis=0, concat_axis=0, tiled=True
        ),
    )
    slot_inputs = recv_inputs.reshape(slot_count, features)
    slot_upstream = recv_upstream.reshape(slot_count, features)
    slot_gates = recv_gates.reshape(slot_count).astype(jnp.float32)
    pre_act = jnp.dot(slot_inputs, gate_full, preferred_element_type=jnp.float32)
    gate_part = pre_act[:, :width]
    up_part = pre_act[:, width:]
    sigma = jax.nn.sigmoid(gate_part)
    activ = gate_part * sigma
    hidden = (activ * up_part).astype(jnp.bfloat16)
    expert_out = product_transposed(hidden, down_full)
    upstream_float = slot_upstream.astype(jnp.float32)
    slot_grad = jnp.sum(upstream_float * expert_out, axis=1).astype(jnp.bfloat16)
    d_expert_out = (slot_gates[:, None] * upstream_float).astype(jnp.bfloat16)
    d_hidden = jnp.dot(d_expert_out, down_full, preferred_element_type=jnp.float32)
    d_gate_part = d_hidden * up_part * sigma * (1.0 + gate_part * (1.0 - sigma))
    d_up_part = d_hidden * activ
    d_pre = jnp.concatenate([d_gate_part, d_up_part], axis=1).astype(jnp.bfloat16)
    d_slot = product_transposed(d_pre, gate_full).astype(jnp.bfloat16)
    down_share = lax.psum_scatter(
        transpose_product(d_expert_out, hidden), "dp", scatter_dimension=0, tiled=True
    )
    back_rows, back_grads = (
        lax.all_to_all(
            d_slot.reshape(groups, CAP, features), "expert", split_axis=0, concat_axis=0, tiled=True
        ),
        lax.all_to_all(
            slot_grad.reshape(groups, CAP), "expert", split_axis=0, concat_axis=0, tiled=True
        ),
    )
    back_rows = back_rows.reshape(slot_count, features)
    back_grads = back_grads.reshape(slot_count)
    grad_tokens = transpose_product(picker, back_rows).astype(jnp.bfloat16)
    gathered_grads = back_grads[jnp.minimum(slot_of, slot_count - 1)]
    grad_gates = jnp.where(inside, gathered_grads, jnp.zeros((), jnp.bfloat16)).reshape(
        tok_rows, TOPK
    )
    return (grad_tokens, grad_gates, down_share[None])


def solution(mesh):
    return jax.shard_map(
        on_device,
        mesh=mesh,
        in_specs=(
            P(("expert", "dp"), None),
            P(("expert", "dp"), None),
            P(("expert", "dp"), None),
            P(("expert", "dp"), None),
            P("expert", "dp", None),
            P("expert", "dp", None),
        ),
        out_specs=(P(("expert", "dp"), None), P(("expert", "dp"), None), P("expert", "dp", None)),
        check_vma=False,
    )
```

profile of v0, /device:TPU:0, one launch (start us, length us, event | category | flops | bytes accessed | tf_op | source)
XLA Modules:
  0.0 151.1 jit_solution(2846326151058442494)
XLA Ops:
  7.2 0.7 all-gather.2.cloned.1.call-update
  7.9 0.8 copy.23
  8.8 1.1 reduce-window.6
  10.6 0.7 broadcast_multiply_fusion
  11.5 0.8 copy.27
  12.5 4.3 %scatter_custom_fusion = s32[48]{0:T(128)S(1)} fusion(s32[1024]{0:T(1024)S(1)} %bitcast.96, s32[1024]{0:T(1024)S(1)} %iota.15, s32[]{:T(128)} %constant.14.clone.1), kind=kCustom, calls=%fused_computation.100 | custom fusion | bytes 196 | tf_op jit(solution)/shard_map/scatter | solution.py:44
  16.9 0.8 gather_fusion
  17.7 0.7 all_to_all.25
  18.3 4.3 %all-to-all-start = ((bf16[4,1,12]{2,1,0:T(2,128)(2,1)}), bf16[4,1,12]{2,1,0:T(2,128)(2,1)S(1)}, u32[]{:S(2)}, u32[]{:S(2)}) async-start(bf16[4,1,12]{2,1,0:T(2,128)(2,1)} %all_to_all.25), calls=%async_computation | async-start | bytes 4096 | tf_op jit(solution)/shard_map/all_to_all | solution.py:72
  22.8 0.7 reshape.156
  23.7 34.8 %all_gather.6 = bf16[1,1024,384]{2,1,0:T(8,128)(2,1)S(1)} all-gather(bf16[1,128,384]{2,1,0:T(8,128)(2,1)S(1)} %copy-done.3), channel_id=1, replica_groups=mesh['expert'=4,'dp'=8] {'dp'}, dimensions={1}, use_global_device_ids=true | all-gather | bytes 884736 | tf_op jit(solution)/shard_map/all_gather | solution.py:25
  58.5 0.7 reshape.157
  59.2 3.3 %all-to-all-start.1 = ((bf16[4,12,1024]{2,1,0:T(8,128)(2,1)}), bf16[4,12,1024]{2,1,0:T(8,128)(2,1)S(1)}, u32[]{:S(2)}, u32[]{:S(2)}) async-start(bf16[4,12,1024]{2,1,0:T(8,128)(2,1)} %reshape.156), calls=%async_computation.1 | async-start | bytes 262144 | tf_op jit(solution)/shard_map/all_to_all | solution.py:65
  62.7 4.5 %all-to-all-done.1 = bf16[4,12,1024]{2,1,0:T(8,128)(2,1)S(1)} async-done(((bf16[4,12,1024]{2,1,0:T(8,128)(2,1)}), bf16[4,12,1024]{2,1,0:T(8,128)(2,1)S(1)}, u32[]{:S(2)}, u32[]{:S(2)}) %all-to-all-start.1) | async-done | bytes 98336 | tf_op jit(solution)/shard_map/all_to_all | solution.py:65
  67.1 3.3 %all-to-all-start.2 = ((bf16[4,12,1024]{2,1,0:T(8,128)(2,1)}), bf16[4,12,1024]{2,1,0:T(8,128)(2,1)S(1)}, u32[]{:S(2)}, u32[]{:S(2)}) async-start(bf16[4,12,1024]{2,1,0:T(8,128)(2,1)} %reshape.157), calls=%async_computation.2 | async-start | bytes 262144 | tf_op jit(solution)/shard_map/all_to_all | solution.py:58
  70.7 4.4 %all-to-all-done.2 = bf16[4,12,1024]{2,1,0:T(8,128)(2,1)S(1)} async-done(((bf16[4,12,1024]{2,1,0:T(8,128)(2,1)}), bf16[4,12,1024]{2,1,0:T(8,128)(2,1)S(1)}, u32[]{:S(2)}, u32[]{:S(2)}) %all-to-all-start.2) | async-done | bytes 98336 | tf_op jit(solution)/shard_map/all_to_all | solution.py:58
  75.1 1.8 %fusion.2 = f32[48,768]{1,0:T(8,128)S(1)} fusion(bf16[48,1024]{1,0:T(8,128)(2,1)S(1)} %reshape.158, bf16[1,1024,768]{2,1,0:T(8,128)(2,1)} %all-gather.2.cloned.1.call-done), kind=kOutput, calls=%fused_computation.4 | convolution fusion | flops 75497472 | bytes 1818624 | tf_op jit(solution)/shard_map/dot_general | solution.py:79
  77.1 1.6 %fusion.11 = f32[1024,384]{1,0:T(8,128)} fusion(bf16[48,384]{1,0:T(8,128)(2,1)S(1)} %get-tuple-element.57, f32[48,1024]{1,0:T(8,128)S(1)} %reshape.163, f32[48]{0:T(128)S(1)} %reshape.164), kind=kOutput, calls=%fused_computation.17 | convolution fusion | flops 37847040 | bytes 1806528 | tf_op jit(solution)/shard_map/dot_general | solution.py:11
  79.2 0.7 convert_element_type.93
  79.9 3.2 %all-to-all-start.4 = ((bf16[4,1,12]{2,1,0:T(2,128)(2,1)}), bf16[4,1,12]{2,1,0:T(2,128)(2,1)S(1)}, u32[]{:S(2)}, u32[]{:S(2)}) async-start(bf16[4,1,12]{2,1,0:T(2,128)(2,1)} %convert_element_type.93), calls=%async_computation.4 | async-start | bytes 4096 | tf_op jit(solution)/shard_map/all_to_all | solution.py:101
  83.1 0.6 fusion.4
  83.7 0.7 reshape.159
  84.4 2.4 %all-to-all-done.4 = bf16[4,1,12]{2,1,0:T(2,128)(2,1)S(1)} async-done(((bf16[4,1,12]{2,1,0:T(2,128)(2,1)}), bf16[4,1,12]{2,1,0:T(2,128)(2,1)S(1)}, u32[]{:S(2)}, u32[]{:S(2)}) %all-to-all-start.4) | async-done | bytes 128 | tf_op jit(solution)/shard_map/all_to_all | solution.py:101
  86.8 3.3 %all-to-all-start.3 = ((bf16[4,12,1024]{2,1,0:T(8,128)(2,1)}), bf16[4,12,1024]{2,1,0:T(8,128)(2,1)S(1)}, u32[]{:S(2)}, u32[]{:S(2)}) async-start(bf16[4,12,1024]{2,1,0:T(8,128)(2,1)} %reshape.159), calls=%async_computation.3 | async-start | bytes 262144 | tf_op jit(solution)/shard_map/all_to_all | solution.py:98
  90.2 0.7 fusion.30
  90.9 0.7 fusion.28
  91.7 0.7 fusion.29
  92.4 4.4 %fusion.24 = (bf16[1024]{0:T(1024)(128)(2,1)S(1)}, s32[1024,1]{0,1:T(1,128)S(1)}) fusion(bf16[]{:T(256)} %bitcast.47, bf16[]{:T(256)} %bitcast.48, bf16[]{:T(256)} %bitcast.49, bf16[]{:T(256)} %bitcast.50, bf16[]{:T(256)} %bitcast.51, bf16[]{:T(256)} %bitcast.53, bf16[]{:T(256)} %bitcast.52, pred[1024,1]{0,1:T(4,128)(4,1)S(1)} %lt.44, ...), kind=kLoop, calls=%fused_computation.93 | loop fusion | flops 18432 | bytes 15374 | tf_op jit(solution)/shard_map/gather | solution.py:108
  97.3 25.7 %select_select_fusion = bf16[1024]{0:T(1024)(128)(2,1)S(1)} fusion(pred[1024]{0:T(1024)(128)(4,1)S(1)} %get-tuple-element.52, pred[1024]{0:T(1024)(128)(4,1)S(1)} %get-tuple-element.51, pred[1024]{0:T(1024)(128)(4,1)S(1)} %get-tuple-element.50, pred[1024]{0:T(1024)(128)(4,1)S(1)} %get-tuple-element.49, pred[1024]{0:T(1024)(128)(4,1)S(1)} %get-tuple-element.48, ...), kind=kLoop, calls=%fused_computation.94 | loop fusion | flops 41984 | bytes 46162 | tf_op jit(solution)/shard_map/gather | solution.py:108
  123.1 0.7 copy.30
  123.8 1.0 convolution_convert_fusion
  124.9 19.4 %reduce-scatter.2.cloned.1.call-done = f32[128,384]{1,0:T(8,128)} async-done(((f32[1024,384]{1,0:T(8,128)}), f32[128,384]{1,0:T(8,128)}) %reduce-scatter.2.cloned.1.call-update) | async-done | bytes 196624 | tf_op jit(solution)/shard_map/reduce_scatter | solution.py:94
  (48 shorter events, 3.4 us)
Async XLA Ops:
  7.2 15.4 %copy-start = (bf16[128,1024]{1,0:T(8,128)(2,1)S(1)}, bf16[128,1024]{1,0:T(8,128)(2,1)}, u32[]{:S(2)}) copy-start(bf16[128,1024]{1,0:T(8,128)(2,1)} %param.7) | copy-start | bytes 786436
  7.2 16.3 %copy-start.2 = (bf16[128,1024]{1,0:T(8,128)(2,1)S(1)}, bf16[128,1024]{1,0:T(8,128)(2,1)}, u32[]{:S(2)}) copy-start(bf16[128,1024]{1,0:T(8,128)(2,1)} %param.6) | copy-start | bytes 786436
  7.2 16.6 %copy-start.3 = (bf16[1,128,384]{2,1,0:T(8,128)(2,1)S(1)}, bf16[1,128,384]{2,1,0:T(8,128)(2,1)}, u32[]{:S(2)}) copy-start(bf16[1,128,384]{2,1,0:T(8,128)(2,1)} %param.11) | copy-start | bytes 294916
  7.2 67.9 %all-gather.2.cloned.1.call-start = ((), (), s32[]{:S(2)}) async-start(), calls=%async_computation.6 | async-start | bytes 1769472 | tf_op jit(solution)/shard_map/all_gather | solution.py:24
  18.3 40.9 %all-to-all-start = ((bf16[4,1,12]{2,1,0:T(2,128)(2,1)}), bf16[4,1,12]{2,1,0:T(2,128)(2,1)S(1)}, u32[]{:S(2)}, u32[]{:S(2)}) async-start(bf16[4,1,12]{2,1,0:T(2,128)(2,1)} %all_to_all.25), calls=%async_computation | async-start | bytes 4096 | tf_op jit(solution)/shard_map/all_to_all | solution.py:72
  59.2 7.9 %all-to-all-start.1 = ((bf16[4,12,1024]{2,1,0:T(8,128)(2,1)}), bf16[4,12,1024]{2,1,0:T(8,128)(2,1)S(1)}, u32[]{:S(2)}, u32[]{:S(2)}) async-start(bf16[4,12,1024]{2,1,0:T(8,128)(2,1)} %reshape.156), calls=%async_computation.1 | async-start | bytes 262144 | tf_op jit(solution)/shard_map/all_to_all | solution.py:65
  67.1 7.9 %all-to-all-start.2 = ((bf16[4,12,1024]{2,1,0:T(8,128)(2,1)}), bf16[4,12,1024]{2,1,0:T(8,128)(2,1)S(1)}, u32[]{:S(2)}, u32[]{:S(2)}) async-start(bf16[4,12,1024]{2,1,0:T(8,128)(2,1)} %reshape.157), calls=%async_computation.2 | async-start | bytes 262144 | tf_op jit(solution)/shard_map/all_to_all | solution.py:58
  70.5 73.8 %reduce-scatter.2.cloned.1.call-start = ((), (), s32[]{:S(2)}) async-start(), calls=%async_computation.7 | async-start | bytes 1769472 | tf_op jit(solution)/shard_map/reduce_scatter | solution.py:94
  78.7 4.4 %copy-start.1 = (bf16[1,1024,768]{2,1,0:T(8,128)(2,1)S(1)}, bf16[1,1024,768]{2,1,0:T(8,128)(2,1)}, u32[]{:S(2)}) copy-start(bf16[1,1024,768]{2,1,0:T(8,128)(2,1)} %all-gather.2.cloned.1.call-done) | copy-start | bytes 4718596
  79.9 6.9 %all-to-all-start.4 = ((bf16[4,1,12]{2,1,0:T(2,128)(2,1)}), bf16[4,1,12]{2,1,0:T(2,128)(2,1)S(1)}, u32[]{:S(2)}, u32[]{:S(2)}) async-start(bf16[4,1,12]{2,1,0:T(2,128)(2,1)} %convert_element_type.93), calls=%async_computation.4 | async-start | bytes 4096 | tf_op jit(solution)/shard_map/all_to_all | solution.py:101
  86.8 37.0 %all-to-all-start.3 = ((bf16[4,12,1024]{2,1,0:T(8,128)(2,1)}), bf16[4,12,1024]{2,1,0:T(8,128)(2,1)S(1)}, u32[]{:S(2)}, u32[]{:S(2)}) async-start(bf16[4,12,1024]{2,1,0:T(8,128)(2,1)} %reshape.159), calls=%async_computation.3 | async-start | bytes 262144 | tf_op jit(solution)/shard_map/all_to_all | solution.py:98
Sparse Core Ops, SparseCore 0:
  10.2 53.8 all-gather.1
  78.9 65.3 reduce-scatter.1
where the time goes:
time: 152 us; the launch traced here: 151 us
  blocking collectives  34.8 us (23%)
  other arithmetic  32.9 us (22%)
  waiting for transfers between devices  31.3 us (21%)
  starting transfers between devices  17.5 us (12%)
  between operations  14.3 us (9%)
  local copies, waits for them, and re-layouts  14.1 us (9%)
  matrix products  6.16 us (4%)
    all_gather x1, blocking collectives, on_device(): lax.all_gather(down_w, 'dp', axis=1, tiled=True)  34.8 us
    gather x3, other arithmetic, on_device(): gathered_grads = back_grads[jnp.minimum(slot_of, slot_count - 1)]  30.6 us
    reduce_scatter x1, waiting for transfers between devices, on_device(): lax.psum_scatter(transpose_product(d_expert_out, hidden), 'dp', scatter_d...  19.4 us
    all_to_all x1, waiting for transfers between devices, on_device(): lax.all_to_all(send_upstream.reshape(groups, CAP, features), 'expert', sp...  4.46 us
    all_to_all x1, waiting for transfers between devices, on_device(): lax.all_to_all(send_inputs.reshape(groups, CAP, features), 'expert', spli...  4.36 us
    scatter x1, local copies, waits for them, and re-layouts, on_device(): owner = jnp.full((slot_count,), -1, jnp.int32).at[slot_of].set(jnp.arange...  4.3 us
    all_to_all x1, starting transfers between devices, on_device(): lax.all_to_all(send_gates.reshape(groups, CAP), 'expert', split_axis=0, c...  4.26 us
    all_to_all x1, starting transfers between devices, on_device(): lax.all_to_all(send_upstream.reshape(groups, CAP, features), 'expert', sp...  3.33 us
  transfers between devices with their start and end apart: 7, of which 4 were waited for; matrix products, arithmetic and copies ran while one was open for 32% of the time, Pallas kernels for 0%

commit v1 on v0

--- a/solution.py
+++ b/solution.py
@@ -5,6 +5,22 @@
 
 TOPK = 8
 CAP = 12
+
+
+def swapped_with_each(value, axis, split, join):
+    ways, here = (lax.axis_size(axis), lax.axis_index(axis))
+    width = value.shape[split] // ways
+    shape = list(value.shape)
+    shape[split] = width
+    height = shape[join]
+    shape[join] = height * ways
+    full = jnp.zeros(shape, value.dtype)
+    for mask in range(ways):
+        part = lax.dynamic_slice_in_dim(value, (here ^ mask) * width, width, axis=split)
+        if mask:
+            part = lax.ppermute(part, axis, [(d, d ^ mask) for d in range(ways)])
+        full = lax.dynamic_update_slice_in_dim(full, part, (here ^ mask) * height, axis=join)
+    return full
 
 
 def transpose_product(left, right):
@@ -62,13 +78,7 @@
             concat_axis=0,
             tiled=True,
         ),
-        lax.all_to_all(
-            send_upstream.reshape(groups, CAP, features),
-            "expert",
-            split_axis=0,
-            concat_axis=0,
-            tiled=True,
-        ),
+        swapped_with_each(send_upstream.reshape(groups, CAP, features), "expert", 0, 0),
         lax.all_to_all(
             send_gates.reshape(groups, CAP), "expert", split_axis=0, concat_axis=0, tiled=True
         ),

time: 152 us -> 145 us (0.954)
  waiting for transfers between devices: 31.3 us -> 26.4 us
    all_to_all x1 -> x0, waiting for transfers between devices: 4.46 us -> none  [on_device(): lax.all_to_all(send_upstream.reshape(groups, CAP, features), 'expert', sp...]
    all_to_all x1 -> x0, starting transfers between devices: 3.33 us -> none  [on_device(): lax.all_to_all(send_upstream.reshape(groups, CAP, features), 'expert', sp...]
    ppermute x0 -> x3, starting transfers between devices: none -> 2.21 us  [swapped_with_each(): part = lax.ppermute(part, axis, [(d, d ^ mask) for d in range(ways)])]
  transfers between devices with their start and end apart: 7 -> 9, of which waited for: 4 -> 3; matrix products, arithmetic and copies ran while one was open for 32% -> 33% of each run, Pallas kernels for 0% -> 0%
where the time goes in v1:
time: 145 us; the launch traced here: 144 us
  blocking collectives  34.4 us (24%)
  other arithmetic  32.9 us (23%)
  waiting for transfers between devices  26.4 us (18%)
  starting transfers between devices  16.4 us (11%)
  between operations  14.4 us (10%)
  local copies, waits for them, and re-layouts  13.5 us (9%)
  matrix products  6.16 us (4%)
    all_gather x1, blocking collectives, on_device(): lax.all_gather(down_w, 'dp', axis=1, tiled=True)  34.4 us
    gather x3, other arithmetic, on_device(): gathered_grads = back_grads[jnp.minimum(slot_of, slot_count - 1)]  30.6 us
    reduce_scatter x1, waiting for transfers between devices, on_device(): lax.psum_scatter(transpose_product(d_expert_out, hidden), 'dp', scatter_d...  19.1 us
    scatter x1, local copies, waits for them, and re-layouts, on_device(): owner = jnp.full((slot_count,), -1, jnp.int32).at[slot_of].set(jnp.arange...  4.3 us
    all_to_all x1, starting transfers between devices, on_device(): lax.all_to_all(send_gates.reshape(groups, CAP), 'expert', split_axis=0, c...  4.26 us
    all_to_all x1, waiting for transfers between devices, on_device(): lax.all_to_all(send_inputs.reshape(groups, CAP, features), 'expert', spli...  4.17 us
    all_to_all x1, starting transfers between devices, on_device(): lax.all_to_all(send_inputs.reshape(groups, CAP, features), 'expert', spli...  3.33 us
    all_to_all x1, starting transfers between devices, on_device(): lax.all_to_all(d_slot.reshape(groups, CAP, features), 'expert', split_axi...  3.33 us
  transfers between devices with their start and end apart: 9, of which 3 were waited for; matrix products, arithmetic and copies ran while one was open for 33% of the time, Pallas kernels for 0%

profile of v1, /device:TPU:0, one launch (start us, length us, event | category | flops | bytes accessed | tf_op | source)
XLA Modules:
  0.0 144.2 jit_solution(6842703474060066222)
XLA Ops:
  7.2 0.7 all-gather.2.cloned.1.call-update
  7.9 0.8 copy.23
  8.7 0.7 broadcast_multiply_fusion
  9.5 1.1 reduce-window.6
  11.5 0.8 copy.27
  12.5 4.3 %scatter_custom_fusion = s32[48]{0:T(128)S(1)} fusion(s32[1024]{0:T(1024)S(1)} %bitcast.96, s32[1024]{0:T(1024)S(1)} %iota.15, s32[]{:T(128)} %constant.16.clone.1), kind=kCustom, calls=%fused_computation.107 | custom fusion | bytes 196 | tf_op jit(solution)/shard_map/scatter | solution.py:60
  16.9 0.8 gather_fusion
  17.7 0.7 all_to_all.21
  18.3 4.3 %all-to-all-start = ((bf16[4,1,12]{2,1,0:T(2,128)(2,1)}), bf16[4,1,12]{2,1,0:T(2,128)(2,1)S(1)}, u32[]{:S(2)}, u32[]{:S(2)}) async-start(bf16[4,1,12]{2,1,0:T(2,128)(2,1)} %all_to_all.21), calls=%async_computation | async-start | bytes 4096 | tf_op jit(solution)/shard_map/all_to_all | solution.py:82
  22.9 0.6 collective-permute-start
  23.5 1.6 %collective-permute-start.1 = (bf16[1,12,1024]{2,1,0:T(8,128)(2,1)S(1)}, bf16[1,12,1024]{2,1,0:T(8,128)(2,1)S(1)}, u32[]{:S(2)}, u32[]{:S(2)}) collective-permute-start(bf16[1,12,1024]{2,1,0:T(8,128)(2,1)S(1)} %get-tuple-element.59), channel_id=1, source_target_pairs={{0,16},{8,24},{16,0},{24,8},{1,17},{9,25},{17,1},{25,9},{2,18},{10... | collective-permute-start | bytes 73736 | tf_op jit(solution)/shard_map/ppermute | solution.py:21
  25.4 34.4 %all_gather.6 = bf16[1,1024,384]{2,1,0:T(8,128)(2,1)S(1)} all-gather(bf16[1,128,384]{2,1,0:T(8,128)(2,1)S(1)} %copy-done.3), channel_id=1, replica_groups=mesh['expert'=4,'dp'=8] {'dp'}, dimensions={1}, use_global_device_ids=true | all-gather | bytes 884736 | tf_op jit(solution)/shard_map/all_gather | solution.py:41
  59.8 0.7 reshape.157
  60.5 3.3 %all-to-all-start.1 = ((bf16[4,12,1024]{2,1,0:T(8,128)(2,1)}), bf16[4,12,1024]{2,1,0:T(8,128)(2,1)S(1)}, u32[]{:S(2)}, u32[]{:S(2)}) async-start(bf16[4,12,1024]{2,1,0:T(8,128)(2,1)} %reshape.157), calls=%async_computation.1 | async-start | bytes 262144 | tf_op jit(solution)/shard_map/all_to_all | solution.py:74
  64.2 4.2 %all-to-all-done.1 = bf16[4,12,1024]{2,1,0:T(8,128)(2,1)S(1)} async-done(((bf16[4,12,1024]{2,1,0:T(8,128)(2,1)}), bf16[4,12,1024]{2,1,0:T(8,128)(2,1)S(1)}, u32[]{:S(2)}, u32[]{:S(2)}) %all-to-all-start.1) | async-done | bytes 98336 | tf_op jit(solution)/shard_map/all_to_all | solution.py:74
  68.5 1.8 %fusion.2 = f32[48,768]{1,0:T(8,128)S(1)} fusion(bf16[48,1024]{1,0:T(8,128)(2,1)S(1)} %reshape.158, bf16[1,1024,768]{2,1,0:T(8,128)(2,1)} %all-gather.2.cloned.1.call-done), kind=kOutput, calls=%fused_computation.4 | convolution fusion | flops 75497472 | bytes 1818624 | tf_op jit(solution)/shard_map/dot_general | solution.py:89
  70.5 1.6 %fusion.11 = f32[1024,384]{1,0:T(8,128)} fusion(bf16[48,384]{1,0:T(8,128)(2,1)S(1)} %get-tuple-element.57, f32[48,1024]{1,0:T(8,128)S(1)} %reshape.163, f32[48]{0:T(128)S(1)} %reshape.164), kind=kOutput, calls=%fused_computation.17 | convolution fusion | flops 37847040 | bytes 1806528 | tf_op jit(solution)/shard_map/dot_general | solution.py:27
  72.6 0.7 convert_element_type.93
  73.3 3.2 %all-to-all-start.3 = ((bf16[4,1,12]{2,1,0:T(2,128)(2,1)}), bf16[4,1,12]{2,1,0:T(2,128)(2,1)S(1)}, u32[]{:S(2)}, u32[]{:S(2)}) async-start(bf16[4,1,12]{2,1,0:T(2,128)(2,1)} %convert_element_type.93), calls=%async_computation.3 | async-start | bytes 4096 | tf_op jit(solution)/shard_map/all_to_all | solution.py:111
  76.5 0.6 fusion.4
  77.1 0.7 reshape.159
  77.8 2.4 %all-to-all-done.3 = bf16[4,1,12]{2,1,0:T(2,128)(2,1)S(1)} async-done(((bf16[4,1,12]{2,1,0:T(2,128)(2,1)}), bf16[4,1,12]{2,1,0:T(2,128)(2,1)S(1)}, u32[]{:S(2)}, u32[]{:S(2)}) %all-to-all-start.3) | async-done | bytes 128 | tf_op jit(solution)/shard_map/all_to_all | solution.py:111
  80.2 3.3 %all-to-all-start.2 = ((bf16[4,12,1024]{2,1,0:T(8,128)(2,1)}), bf16[4,12,1024]{2,1,0:T(8,128)(2,1)S(1)}, u32[]{:S(2)}, u32[]{:S(2)}) async-start(bf16[4,12,1024]{2,1,0:T(8,128)(2,1)} %reshape.159), calls=%async_computation.2 | async-start | bytes 262144 | tf_op jit(solution)/shard_map/all_to_all | solution.py:108
  83.6 0.7 fusion.30
  84.3 0.7 fusion.28
  85.0 0.7 fusion.29
  85.8 4.4 %fusion.24 = (bf16[1024]{0:T(1024)(128)(2,1)S(1)}, s32[1024,1]{0,1:T(1,128)S(1)}) fusion(bf16[]{:T(256)} %bitcast.47, bf16[]{:T(256)} %bitcast.48, bf16[]{:T(256)} %bitcast.49, bf16[]{:T(256)} %bitcast.50, bf16[]{:T(256)} %bitcast.51, bf16[]{:T(256)} %bitcast.53, bf16[]{:T(256)} %bitcast.52, pred[1024,1]{0,1:T(4,128)(4,1)S(1)} %lt.60, ...), kind=kLoop, calls=%fused_computation.94 | loop fusion | flops 18432 | bytes 15374 | tf_op jit(solution)/shard_map/gather | solution.py:118
  90.2 0.5 compare_reduce_fusion.40
  90.7 25.7 %select_select_fusion = bf16[1024]{0:T(1024)(128)(2,1)S(1)} fusion(pred[1024]{0:T(1024)(128)(4,1)S(1)} %get-tuple-element.52, pred[1024]{0:T(1024)(128)(4,1)S(1)} %get-tuple-element.51, pred[1024]{0:T(1024)(128)(4,1)S(1)} %get-tuple-element.50, pred[1024]{0:T(1024)(128)(4,1)S(1)} %get-tuple-element.49, pred[1024]{0:T(1024)(128)(4,1)S(1)} %get-tuple-element.48, ...), kind=kLoop, calls=%fused_computation.95 | loop fusion | flops 41984 | bytes 46162 | tf_op jit(solution)/shard_map/gather | solution.py:118
  116.5 0.7 copy.30
  117.2 1.0 convolution_convert_fusion
  118.3 19.1 %reduce-scatter.2.cloned.1.call-done = f32[128,384]{1,0:T(8,128)} async-done(((f32[1024,384]{1,0:T(8,128)}), f32[128,384]{1,0:T(8,128)}) %reduce-scatter.2.cloned.1.call-update) | async-done | bytes 196624 | tf_op jit(solution)/shard_map/reduce_scatter | solution.py:104
  (57 shorter events, 3.0 us)
Async XLA Ops:
  7.2 15.4 %copy-start = (bf16[128,1024]{1,0:T(8,128)(2,1)S(1)}, bf16[128,1024]{1,0:T(8,128)(2,1)}, u32[]{:S(2)}) copy-start(bf16[128,1024]{1,0:T(8,128)(2,1)} %param.7) | copy-start | bytes 786436
  7.2 18.0 %copy-start.2 = (bf16[128,1024]{1,0:T(8,128)(2,1)S(1)}, bf16[128,1024]{1,0:T(8,128)(2,1)}, u32[]{:S(2)}) copy-start(bf16[128,1024]{1,0:T(8,128)(2,1)} %param.6) | copy-start | bytes 786436
  7.2 18.2 %copy-start.3 = (bf16[1,128,384]{2,1,0:T(8,128)(2,1)S(1)}, bf16[1,128,384]{2,1,0:T(8,128)(2,1)}, u32[]{:S(2)}) copy-start(bf16[1,128,384]{2,1,0:T(8,128)(2,1)} %param.11) | copy-start | bytes 294916
  7.2 61.2 %all-gather.2.cloned.1.call-start = ((), (), s32[]{:S(2)}) async-start(), calls=%async_computation.5 | async-start | bytes 1769472 | tf_op jit(solution)/shard_map/all_gather | solution.py:40
  18.3 42.2 %all-to-all-start = ((bf16[4,1,12]{2,1,0:T(2,128)(2,1)}), bf16[4,1,12]{2,1,0:T(2,128)(2,1)S(1)}, u32[]{:S(2)}, u32[]{:S(2)}) async-start(bf16[4,1,12]{2,1,0:T(2,128)(2,1)} %all_to_all.21), calls=%async_computation | async-start | bytes 4096 | tf_op jit(solution)/shard_map/all_to_all | solution.py:82
  22.9 41.1 %collective-permute-start = (bf16[1,12,1024]{2,1,0:T(8,128)(2,1)S(1)}, bf16[1,12,1024]{2,1,0:T(8,128)(2,1)S(1)}, u32[]{:S(2)}, u32[]{:S(2)}) collective-permute-start(bf16[1,12,1024]{2,1,0:T(8,128)(2,1)S(1)} %get-tuple-element.60), channel_id=1, source_target_pairs={{0,8},{8,0},{16,24},{24,16},{1,9},{9,1},{17,25},{25,17},{2,10},{10... | collective-permute-start | bytes 73736 | tf_op jit(solution)/shard_map/ppermute | solution.py:21
  23.5 40.5 %collective-permute-start.1 = (bf16[1,12,1024]{2,1,0:T(8,128)(2,1)S(1)}, bf16[1,12,1024]{2,1,0:T(8,128)(2,1)S(1)}, u32[]{:S(2)}, u32[]{:S(2)}) collective-permute-start(bf16[1,12,1024]{2,1,0:T(8,128)(2,1)S(1)} %get-tuple-element.59), channel_id=1, source_target_pairs={{0,16},{8,24},{16,0},{24,8},{1,17},{9,25},{17,1},{25,9},{2,18},{10... | collective-permute-start | bytes 73736 | tf_op jit(solution)/shard_map/ppermute | solution.py:21
  25.1 38.9 %collective-permute-start.2 = (bf16[1,12,1024]{2,1,0:T(8,128)(2,1)S(1)}, bf16[1,12,1024]{2,1,0:T(8,128)(2,1)S(1)}, u32[]{:S(2)}, u32[]{:S(2)}) collective-permute-start(bf16[1,12,1024]{2,1,0:T(8,128)(2,1)S(1)} %get-tuple-element.58), channel_id=1, source_target_pairs={{0,24},{8,16},{16,8},{24,0},{1,25},{9,17},{17,9},{25,1},{2,26},{10... | collective-permute-start | bytes 73736 | tf_op jit(solution)/shard_map/ppermute | solution.py:21
  60.5 7.9 %all-to-all-start.1 = ((bf16[4,12,1024]{2,1,0:T(8,128)(2,1)}), bf16[4,12,1024]{2,1,0:T(8,128)(2,1)S(1)}, u32[]{:S(2)}, u32[]{:S(2)}) async-start(bf16[4,12,1024]{2,1,0:T(8,128)(2,1)} %reshape.157), calls=%async_computation.1 | async-start | bytes 262144 | tf_op jit(solution)/shard_map/all_to_all | solution.py:74
  63.8 73.6 %reduce-scatter.2.cloned.1.call-start = ((), (), s32[]{:S(2)}) async-start(), calls=%async_computation.6 | async-start | bytes 1769472 | tf_op jit(solution)/shard_map/reduce_scatter | solution.py:104
  72.1 4.4 %copy-start.1 = (bf16[1,1024,768]{2,1,0:T(8,128)(2,1)S(1)}, bf16[1,1024,768]{2,1,0:T(8,128)(2,1)}, u32[]{:S(2)}) copy-start(bf16[1,1024,768]{2,1,0:T(8,128)(2,1)} %all-gather.2.cloned.1.call-done) | copy-start | bytes 4718596
  73.3 6.9 %all-to-all-start.3 = ((bf16[4,1,12]{2,1,0:T(2,128)(2,1)}), bf16[4,1,12]{2,1,0:T(2,128)(2,1)S(1)}, u32[]{:S(2)}, u32[]{:S(2)}) async-start(bf16[4,1,12]{2,1,0:T(2,128)(2,1)} %convert_element_type.93), calls=%async_computation.3 | async-start | bytes 4096 | tf_op jit(solution)/shard_map/all_to_all | solution.py:111
  80.2 37.0 %all-to-all-start.2 = ((bf16[4,12,1024]{2,1,0:T(8,128)(2,1)}), bf16[4,12,1024]{2,1,0:T(8,128)(2,1)S(1)}, u32[]{:S(2)}, u32[]{:S(2)}) async-start(bf16[4,12,1024]{2,1,0:T(8,128)(2,1)} %reshape.159), calls=%async_computation.2 | async-start | bytes 262144 | tf_op jit(solution)/shard_map/all_to_all | solution.py:108
Sparse Core Ops, SparseCore 0:
  10.2 54.8 all-gather.1
  72.3 65.0 reduce-scatter.1
